TPU v7x, 32 devices: a whole 2x2x4 slice. The times are simulated.
32 devices in a mesh: wide: 8 (over z, y), narrow: 4 (over x, core).
Axes of the slice: x: 2, y: 2, z: 4, core: 2. Of those that a mesh axis runs over, the one named last changes fastest.
Arguments:
- desc_a: bfloat16 [4096, 128], P('wide'), may hold values from -6 to 6
- desc_b: bfloat16 [32768, 128], P('narrow'), may hold values from -6 to 6
- logmass_a: float32 [4096], P('wide'), may hold values from -6 to 6
- logmass_b: float32 [32768], P('narrow'), may hold values from -6 to 6
- g_start: float32 [32768], P('narrow'), may hold values from -1 to 16, as said below
Outputs:
- potential_a: float32 [4096], P('wide')
- potential_b: float32 [32768], P('narrow')
- flow_a: float32 [4096, 128], P('wide')
- flow_b: float32 [32768, 128], P(('narrow', 'wide'))
Inputs may be any that keep to these rules, and one draw needn't show every extreme that they name: `g_start`: potentials of view B carried over from the previous pair of views.
All inputs are finite; a program needn't handle non-finite values.
Results may differ from a plain program's by a relative error of at most 0.01.
Values may be sent and summed in bfloat16 or wider, within the bound.
A program may use at most 64 MiB of HBM per device.

v0:
```python
import jax
import jax.numpy as jnp
from jax import lax
from jax.sharding import PartitionSpec as P

ITERS = 2
EPS = 0.05


def combined_all(part, axis, combine):
    gathered = jax.tree.map(lambda a: lax.all_gather(a, axis), part)

    def take(source):
        return jax.tree.map(lambda a: lax.dynamic_index_in_dim(a, source, 0, False), gathered)

    return lax.fori_loop(
        1, lax.axis_size(axis), lambda source, state: combine(state, take(source)), take(0)
    )


def unit_rows(desc):
    wide32 = desc.astype(jnp.float32)
    return (wide32 / jnp.sqrt(jnp.sum(wide32 * wide32, axis=1, keepdims=True) + 1e-06)).astype(
        jnp.bfloat16
    )


def cost_of(left, right):
    return 2.0 - 2.0 * lax.dot_general(
        left, right, (((1,), (1,)), ((), ())), preferred_element_type=jnp.float32
    )


def left_product(weights, tile_a):
    return lax.dot_general(
        weights, tile_a, (((0,), (0,)), ((), ())), preferred_element_type=jnp.float32
    )


def pair_combine(first_pair, second_pair):
    new_high = jnp.maximum(first_pair[0], second_pair[0])
    summed = first_pair[1] * jnp.exp(first_pair[0] - new_high) + second_pair[1] * jnp.exp(
        second_pair[0] - new_high
    )
    return (new_high, summed)


def finish_rows(highest, summed):
    highest, summed = combined_all((highest, summed), "narrow", pair_combine)
    return highest + jnp.log(summed)


def finish_cols(highest, summed):
    highest, summed = combined_all((highest, summed), "wide", pair_combine)
    return highest + jnp.log(summed)


def row_update(state_now, pot_part, cost):
    highest, summed = state_now
    scores = (pot_part[None, :] - cost) / EPS
    new_high = jnp.maximum(highest, jnp.max(scores, axis=1))
    summed = summed * jnp.exp(highest - new_high) + jnp.sum(
        jnp.exp(scores - new_high[:, None]), axis=1
    )
    return (new_high, summed)


def on_device(desc_a, desc_b, logmass_a, logmass_b, g_start):
    unit_a = unit_rows(desc_a)
    unit_b = unit_rows(desc_b)
    n_rows, feat_width = unit_a.shape
    n_cols = unit_b.shape[0]
    col_span = min(n_cols, 2048)
    n_tiles = n_cols // col_span
    b_tiles = unit_b.reshape(n_tiles, col_span, feat_width)
    row_init = (jnp.full((n_rows,), -jnp.inf, jnp.float32), jnp.zeros((n_rows,), jnp.float32))

    def row_partial(potential):

        def row_one_tile(state_now, inputs):
            tile_b, pot_part = inputs
            return (row_update(state_now, pot_part, cost_of(unit_a, tile_b)), None)

        result, _ = lax.scan(
            row_one_tile, row_init, (b_tiles, potential.reshape(n_tiles, col_span))
        )
        return result

    potential_b = g_start
    for sweep_index in range(ITERS):
        row_pot = EPS * logmass_a - EPS * finish_rows(*row_partial(potential_b))

        def col_one_tile(tile_b):
            scores = (row_pot[:, None] - cost_of(unit_a, tile_b)) / EPS
            highest = jnp.max(scores, axis=0)
            return (highest, jnp.sum(jnp.exp(scores - highest[None, :]), axis=0))

        highest, summed = lax.map(col_one_tile, b_tiles)
        lse_b = finish_cols(*(highest.reshape(n_cols), summed.reshape(n_cols)))
        potential_b = EPS * logmass_b - EPS * lse_b
    my_share = n_cols // lax.axis_size("wide")
    first_row = lax.axis_index("wide") * my_share
    own_cols = lax.dynamic_slice_in_dim(unit_b, first_row, my_share, 0)

    def joint_tile(state_now, inputs):
        tile_b, pot_part, lse_part = inputs
        cost = cost_of(unit_a, tile_b)
        weights = jnp.exp((row_pot[:, None] - cost) / EPS - lse_part[None, :]).astype(jnp.bfloat16)
        return (row_update(state_now, pot_part, cost), left_product(weights, unit_a))

    row_stats, tile_sums = lax.scan(
        joint_tile,
        row_init,
        (b_tiles, potential_b.reshape(n_tiles, col_span), lse_b.reshape(n_tiles, col_span)),
    )
    lse_a = finish_rows(*row_stats)
    sums_b = lax.psum_scatter(
        tile_sums.reshape(n_cols, feat_width).astype(jnp.bfloat16),
        "wide",
        scatter_dimension=0,
        tiled=True,
    ).astype(jnp.float32)
    flow_b = sums_b - own_cols.astype(jnp.float32)
    potential_a = EPS * logmass_a - EPS * lse_a

    def flow_tile(acc_now, inputs):
        tile_b, pot_part = inputs
        weights = jnp.exp(
            (pot_part[None, :] - cost_of(unit_a, tile_b)) / EPS - lse_a[:, None]
        ).astype(jnp.bfloat16)
        return (acc_now + jnp.dot(weights, tile_b, preferred_element_type=jnp.float32), None)

    sums_a, _ = lax.scan(
        flow_tile,
        jnp.zeros((n_rows, feat_width), jnp.float32),
        (b_tiles, potential_b.reshape(n_tiles, col_span)),
    )
    sums_a = lax.psum(sums_a.astype(jnp.bfloat16), "narrow").astype(jnp.float32)
    flow_a = sums_a - unit_a.astype(jnp.float32)
    return (potential_a, potential_b, flow_a, flow_b)


def solution(mesh):
    return jax.shard_map(
        on_device,
        mesh=mesh,
        in_specs=(P("wide", None), P("narrow", None), P("wide"), P("narrow"), P("narrow")),
        out_specs=(P("wide"), P("narrow"), P("wide", None), P(("narrow", "wide"), None)),
        check_vma=False,
    )
```

profile of v0, /device:TPU:0, one launch (start us, length us, event | category | flops | bytes accessed | tf_op | source)
XLA Modules:
  0.0 360.6 jit_solution(10728813550272672152)
XLA Ops:
  8.1 2.7 fusion.36
  10.9 4.6 %fusion.37 = bf16[8192,128]{1,0:T(8,128)(2,1)S(1)} fusion(bf16[8192,128]{1,0:T(8,128)(2,1)} %param.28, f32[8192]{0:T(1024)S(1)} %add_sqrt_fusion), kind=kLoop, calls=%fused_computation.76 | loop fusion | flops 3145728 | bytes 4227072 | tf_op jit(solution)/shard_map/convert_element_type | solution.py:23
  15.8 22.7 %while.168 = (s32[]{:T(128)}, f32[512]{0:T(512)S(1)}, f32[512]{0:T(512)S(1)}, f32[4,2048]{1,0:T(4,128)S(1)}, bf16[4,2048,128]{2,1,0:T(8,128)(2,1)S(1)}, /*index=5*/bf16[512,128]{1,0:T(8,128)(2,1)S(1)}, s32[]{:T(128)}, s32[]{:T(128)}) while((s32[]{:T(128)}, f32[512]{0:T(512)S(1)}, f32[512]{0:T(512)S(1)}, f32[4,2048]{1,0:T(4,128)S(1)}, ...), condition=%wide.region_5.6_spmd.clone, body=%wide.region_2.5_spmd.clone.sunk | while | flops 275778048 | bytes 9095272 | solution.py:84
  15.9 2.8 fusion.75
  18.7 2.8 exponential_reduce_fusion.12
  21.5 2.8 fusion.75
  24.3 2.8 exponential_reduce_fusion.12
  27.2 2.8 fusion.75
  30.0 2.8 exponential_reduce_fusion.12
  32.9 2.8 fusion.75
  35.7 2.8 exponential_reduce_fusion.12
  38.5 6.2 %all-gather.6 = f32[4,1,512]{2,1,0:T(1,128)S(1)} all-gather(f32[1,1,512]{2,1,0:T(1,128)S(1)} %bitcast.198), channel_id=2, replica_groups=mesh['wide'=8,'narrow'=4] {'narrow'}, dimensions={0}, use_global_device_ids=true | all-gather | bytes 10240 | tf_op jit(solution)/shard_map/all_gather | solution.py:11
  44.7 5.5 %all-gather.7 = f32[4,1,512]{2,1,0:T(1,128)S(1)} all-gather(f32[1,1,512]{2,1,0:T(1,128)S(1)} %bitcast.217), channel_id=3, replica_groups=mesh['wide'=8,'narrow'=4] {'narrow'}, dimensions={0}, use_global_device_ids=true | all-gather | bytes 10240 | tf_op jit(solution)/shard_map/all_gather | solution.py:11
  50.4 7.3 %while.162 = (s32[]{:T(128)}, f32[4,2048]{1,0:T(4,128)S(1)}, f32[4,2048]{1,0:T(4,128)S(1)}, f32[512]{0:T(512)S(1)}, bf16[4,2048,128]{2,1,0:T(8,128)(2,1)S(1)}, /...) while((s32[]{:T(128)}, f32[4,2048]{1,0:T(4,128)S(1)}, f32[4,2048]{1,0:T(4,128)S(1)}, ...), condition=%wide.region_11.12_spmd, body=%wide.region_8.11_spmd.sunk | while | flops 275771392 | bytes 9103457 | solution.py:98
  50.4 0.9 fusion.71
  52.2 0.9 fusion.71
  54.1 0.9 fusion.71
  55.9 0.9 fusion.71
  57.8 31.4 %all-gather.8 = f32[8,1,8192]{2,1,0:T(1,128)S(1)} all-gather(f32[1,1,8192]{2,1,0:T(1,128)S(1)} %reshape.74), channel_id=1, replica_groups=mesh['wide'=8,'narrow'=4] {'wide'}, dimensions={0}, use_global_device_ids=true | all-gather | bytes 294912 | tf_op jit(solution)/shard_map/all_gather | solution.py:11
  89.4 30.7 %all-gather.9 = f32[8,1,8192]{2,1,0:T(1,128)S(1)} all-gather(f32[1,1,8192]{2,1,0:T(1,128)S(1)} %reshape.76), channel_id=1, replica_groups=mesh['wide'=8,'narrow'=4] {'wide'}, dimensions={0}, use_global_device_ids=true | all-gather | bytes 294912 | tf_op jit(solution)/shard_map/all_gather | solution.py:11
  120.3 0.8 while.163
  121.2 22.7 %while.169 = (s32[]{:T(128)}, f32[512]{0:T(512)S(1)}, f32[512]{0:T(512)S(1)}, f32[4,2048]{1,0:T(4,128)S(1)}, bf16[4,2048,128]{2,1,0:T(8,128)(2,1)S(1)}, /*index=5*/bf16[512,128]{1,0:T(8,128)(2,1)S(1)}, s32[]{:T(128)}, s32[]{:T(128)}) while((s32[]{:T(128)}, f32[512]{0:T(512)S(1)}, f32[512]{0:T(512)S(1)}, ...), condition=%wide.region_17.18_spmd.clone, body=%wide.region_14.17_spmd.clone.sunk | while | flops 275778048 | bytes 9095272 | solution.py:84
  121.3 2.8 fusion.78
  124.1 2.8 exponential_reduce_fusion.13
  126.9 2.8 fusion.78
  129.7 2.8 exponential_reduce_fusion.13
  132.6 2.8 fusion.78
  135.4 2.8 exponential_reduce_fusion.13
  138.3 2.8 fusion.78
  141.1 2.8 exponential_reduce_fusion.13
  143.9 5.2 %all-gather.10 = f32[4,1,512]{2,1,0:T(1,128)S(1)} all-gather(f32[1,1,512]{2,1,0:T(1,128)S(1)} %bitcast.197), channel_id=4, replica_groups=mesh['wide'=8,'narrow'=4] {'narrow'}, dimensions={0}, use_global_device_ids=true | all-gather | bytes 10240 | tf_op jit(solution)/shard_map/all_gather | solution.py:11
  149.1 5.2 %all-gather.11 = f32[4,1,512]{2,1,0:T(1,128)S(1)} all-gather(f32[1,1,512]{2,1,0:T(1,128)S(1)} %bitcast.216), channel_id=5, replica_groups=mesh['wide'=8,'narrow'=4] {'narrow'}, dimensions={0}, use_global_device_ids=true | all-gather | bytes 10240 | tf_op jit(solution)/shard_map/all_gather | solution.py:11
  154.5 7.3 %while.165 = (s32[]{:T(128)}, f32[4,2048]{1,0:T(4,128)S(1)}, f32[4,2048]{1,0:T(4,128)S(1)}, f32[512]{0:T(512)S(1)}, bf16[4,2048,128]{2,1,0:T(8,128)(2,1)S(1)}, /...) while((s32[]{:T(128)}, f32[4,2048]{1,0:T(4,128)S(1)}, f32[4,2048]{1,0:T(4,128)S(1)}, ...), condition=%wide.region_23.24_spmd, body=%wide.region_20.23_spmd.sunk | while | flops 275771392 | bytes 9103457 | solution.py:98
  154.5 0.9 fusion.73
  156.3 0.9 fusion.73
  158.2 0.9 fusion.73
  160.0 0.9 fusion.73
  161.8 30.8 %all-gather.12 = f32[8,1,8192]{2,1,0:T(1,128)S(1)} all-gather(f32[1,1,8192]{2,1,0:T(1,128)S(1)} %reshape.82), channel_id=1, replica_groups=mesh['wide'=8,'narrow'=4] {'wide'}, dimensions={0}, use_global_device_ids=true | all-gather | bytes 294912 | tf_op jit(solution)/shard_map/all_gather | solution.py:11
  192.9 30.9 %all-gather.13 = f32[8,1,8192]{2,1,0:T(1,128)S(1)} all-gather(f32[1,1,8192]{2,1,0:T(1,128)S(1)} %reshape.84), channel_id=1, replica_groups=mesh['wide'=8,'narrow'=4] {'wide'}, dimensions={0}, use_global_device_ids=true | all-gather | bytes 294912 | tf_op jit(solution)/shard_map/all_gather | solution.py:11
  224.0 0.8 while.166
  225.5 32.9 %while.170 = (s32[]{:T(128)}, f32[512]{0:T(512)S(1)}, f32[512]{0:T(512)S(1)}, bf16[4,2048,128]{2,1,0:T(8,128)(2,1)}, f32[4,2048]{1,0:T(4,128)S(1)}, /*index=5*/b...) while((s32[]{:T(128)}, f32[512]{0:T(512)S(1)}, ...), condition=%wide.region_29.30_spmd.clone, body=%wide.region_26.29_spmd.clone.sunk | while | flops 554699264 | bytes 31281820 | solution.py:111
  225.5 2.7 fusion.82
  228.2 3.1 exponential_reduce_fusion.14
  231.7 2.0 fusion.84
  233.7 2.7 fusion.82
  236.5 3.1 exponential_reduce_fusion.14
  239.9 2.1 fusion.84
  242.0 2.7 fusion.82
  244.7 3.1 exponential_reduce_fusion.14
  248.2 2.0 fusion.84
  250.2 2.7 fusion.82
  252.9 3.1 exponential_reduce_fusion.14
  256.4 2.1 fusion.84
  258.4 5.2 %all-gather.14 = f32[4,1,512]{2,1,0:T(1,128)S(1)} all-gather(f32[1,1,512]{2,1,0:T(1,128)S(1)} %bitcast.196), channel_id=6, replica_groups=mesh['wide'=8,'narrow'=4] {'narrow'}, dimensions={0}, use_global_device_ids=true | all-gather | bytes 10240 | tf_op jit(solution)/shard_map/all_gather | solution.py:11
  263.6 5.2 %all-gather.15 = f32[4,1,512]{2,1,0:T(1,128)S(1)} all-gather(f32[1,1,512]{2,1,0:T(1,128)S(1)} %bitcast.215), channel_id=7, replica_groups=mesh['wide'=8,'narrow'=4] {'narrow'}, dimensions={0}, use_global_device_ids=true | all-gather | bytes 10240 | tf_op jit(solution)/shard_map/all_gather | solution.py:11
  269.6 7.1 %while.171 = (s32[]{:T(128)}, f32[512,128]{1,0:T(8,128)S(1)}, f32[4,2048]{1,0:T(4,128)S(1)}, bf16[4,2048,128]{2,1,0:T(8,128)(2,1)S(1)}, bf16[512,128]{1,0:T(8,12...) while((s32[]{:T(128)}, f32[512,128]{1,0:T(8,128)S(1)}, f32[4,2048]{1,0:T(4,128)S(1)}, ...), condition=%wide.region_33.34_spmd.clone, body=%wide.region_32.33_spmd.clone.sunk | while | flops 543293440 | bytes 1731683 | solution.py:133
  269.6 1.7 fusion.88
  271.3 1.7 fusion.88
  273.1 1.7 fusion.88
  274.9 1.7 fusion.88
  277.9 32.1 %all-reduce.2.cloned.1.call-done = bf16[512,128]{1,0:T(8,128)(2,1)} async-done(((bf16[512,128]{1,0:T(8,128)(2,1)}), bf16[512,128]{1,0:T(8,128)(2,1)}) %all-reduce.2.cloned.1.call-update) | async-done | bytes 131088 | tf_op jit(solution)/shard_map/psum | solution.py:138
  310.0 1.7 convert_subtract_fusion.1
  311.7 39.6 %reduce-scatter.2.cloned.1.call-done = bf16[1024,128]{1,0:T(8,128)(2,1)} async-done(((bf16[8192,128]{1,0:T(8,128)(2,1)}), bf16[1024,128]{1,0:T(8,128)(2,1)}) %reduce-scatter.2.cloned.1.call-update) | async-done | bytes 262160 | tf_op jit(solution)/shard_map/reduce_scatter | solution.py:117
  351.4 1.8 convert_subtract_fusion
  (197 shorter events, 14.9 us)
Async XLA Ops:
  8.0 7.5 %copy-start.1 = (bf16[512,128]{1,0:T(8,128)(2,1)S(1)}, bf16[512,128]{1,0:T(8,128)(2,1)}, u32[]{:S(2)}) copy-start(bf16[512,128]{1,0:T(8,128)(2,1)} %param.27) | copy-start | bytes 393220
  8.0 7.8 %copy-start.4 = (f32[8192]{0:T(1024)S(1)}, f32[8192]{0:T(1024)}, u32[]{:S(2)}) copy-start(f32[8192]{0:T(1024)} %param.31) | copy-start | bytes 98308
  8.0 302.0 %all-reduce.2.cloned.1.call-start = ((), (), s32[]{:S(2)}) async-start(), calls=%async_computation.1 | async-start | bytes 262144 | tf_op jit(solution)/shard_map/psum | solution.py:138
  15.8 34.5 %copy-start.5 = (f32[512]{0:T(512)S(1)}, f32[512]{0:T(512)}, u32[]{:S(2)}) copy-start(f32[512]{0:T(512)} %param.29) | copy-start | bytes 6148
  50.4 70.8 %copy-start.3 = (f32[8192]{0:T(1024)S(1)}, f32[8192]{0:T(1024)}, u32[]{:S(2)}) copy-start(f32[8192]{0:T(1024)} %param.30) | copy-start | bytes 98308
  224.9 0.6 copy-start.2
  228.2 3.4 copy-start
  236.5 3.4 copy-start
  244.7 3.4 copy-start
  252.9 3.4 copy-start
  277.3 74.1 %reduce-scatter.2.cloned.1.call-start = ((), (), s32[]{:S(2)}) async-start(), calls=%async_computation.2 | async-start | bytes 2359296 | tf_op jit(solution)/shard_map/reduce_scatter | solution.py:117
Sparse Core Ops, SparseCore 0:
  277.4 32.4 all-reduce.1
Sparse Core Ops, SparseCore 1:
  281.3 70.0 reduce-scatter.1
where the time goes:
time: 361 us
  blocking collectives  156 us (43%)
  waiting for transfers between devices  72.3 us (20%)
  matrix products  55.3 us (15%)
  other arithmetic  53.4 us (15%)
  between operations  15.9 us (4%)
  local copies, waits for them, and re-layouts  6.07 us (2%)
    all_gather x10, blocking collectives, combined_all(): gathered = jax.tree.map(lambda a: lax.all_gather(a, axis), part)  156 us
    dot_general x20, matrix products, cost_of(): lax.dot_general(left, right, (((1,), (1,)), ((), ())), preferred_element_...  40.2 us
    reduce_scatter x1, waiting for transfers between devices, on_device(): lax.psum_scatter(tile_sums.reshape(n_cols, feat_width).astype(jnp.bfloat1...  39.6 us
    reduce_sum x12, other arithmetic, row_update(): jnp.sum(jnp.exp(scores - new_high[:, None]), axis=1)  34.8 us
    psum x1, waiting for transfers between devices, on_device(): sums_a = lax.psum(sums_a.astype(jnp.bfloat16), 'narrow').astype(jnp.float32)  32.1 us
    dot_general x4, matrix products, left_product(): lax.dot_general(weights, tile_a, (((0,), (0,)), ((), ())), preferred_elem...  8.21 us
  transfers between devices with their start and end apart: 2, of which 2 were waited for; matrix products, arithmetic and copies ran while one was open for 0% of the time, Pallas kernels for 0%

commit v1 on v0

--- a/solution.py
+++ b/solution.py
@@ -5,6 +5,12 @@
 
 ITERS = 2
 EPS = 0.05
+
+
+def add_all(block, mesh_axis):
+    parts = lax.all_gather(block, mesh_axis, axis=0, tiled=False)
+    result = parts.sum(axis=0)
+    return result
 
 
 def combined_all(part, axis, combine):
@@ -135,7 +141,7 @@
         jnp.zeros((n_rows, feat_width), jnp.float32),
         (b_tiles, potential_b.reshape(n_tiles, col_span)),
     )
-    sums_a = lax.psum(sums_a.astype(jnp.bfloat16), "narrow").astype(jnp.float32)
+    sums_a = add_all(sums_a.astype(jnp.bfloat16), "narrow").astype(jnp.float32)
     flow_a = sums_a - unit_a.astype(jnp.float32)
     return (potential_a, potential_b, flow_a, flow_b)
 

time: 361 us -> 337 us (0.934)
  waiting for transfers between devices: 72.3 us -> 43.3 us
  blocking collectives: 156 us -> 164 us
    psum x1 -> x0, waiting for transfers between devices: 32.1 us -> none  [on_device(): sums_a = lax.psum(sums_a.astype(jnp.bfloat16), 'narrow').astype(jnp.float32)]
    all_gather x0 -> x1, blocking collectives: none -> 7.3 us  [add_all(): parts = lax.all_gather(block, mesh_axis, axis=0, tiled=False)]
  transfers between devices with their start and end apart: 2 -> 1, of which waited for: 2 -> 1; matrix products, arithmetic and copies ran while one was open for 0% -> 3% of each run, Pallas kernels for 0% -> 0%
where the time goes in v1:
time: 337 us; the launch traced here: 336 us
  blocking collectives  164 us (49%)
  matrix products  55.3 us (16%)
  other arithmetic  52 us (15%)
  waiting for transfers between devices  43.3 us (13%)
  between operations  14.4 us (4%)
  local copies, waits for them, and re-layouts  6.07 us (2%)
    all_gather x10, blocking collectives, combined_all(): gathered = jax.tree.map(lambda a: lax.all_gather(a, axis), part)  156 us
    reduce_scatter x1, waiting for transfers between devices, on_device(): lax.psum_scatter(tile_sums.reshape(n_cols, feat_width).astype(jnp.bfloat1...  43.2 us
    dot_general x20, matrix products, cost_of(): lax.dot_general(left, right, (((1,), (1,)), ((), ())), preferred_element_...  40.2 us
    reduce_sum x12, other arithmetic, row_update(): jnp.sum(jnp.exp(scores - new_high[:, None]), axis=1)  34.8 us
    dot_general x4, matrix products, left_product(): lax.dot_general(weights, tile_a, (((0,), (0,)), ((), ())), preferred_elem...  8.25 us
    all_gather x1, blocking collectives, add_all(): parts = lax.all_gather(block, mesh_axis, axis=0, tiled=False)  7.3 us
    dot_general x4, matrix products, flow_tile(): jnp.dot(weights, tile_b, preferred_element_type=jnp.float32)  6.86 us
  transfers between devices with their start and end apart: 1, of which 1 were waited for; matrix products, arithmetic and copies ran while one was open for 3% of the time, Pallas kernels for 0%

profile of v1, /device:TPU:0, one launch (start us, length us, event | category | flops | bytes accessed | tf_op | source)
XLA Modules:
  0.0 335.9 jit_solution(12819288322962061409)
XLA Ops:
  7.2 2.7 fusion.36
  10.0 4.6 %fusion.37 = bf16[8192,128]{1,0:T(8,128)(2,1)S(1)} fusion(bf16[8192,128]{1,0:T(8,128)(2,1)} %param.28, f32[8192]{0:T(1024)S(1)} %add_sqrt_fusion), kind=kLoop, calls=%fused_computation.76 | loop fusion | flops 3145728 | bytes 4227072 | tf_op jit(solution)/shard_map/convert_element_type | solution.py:29
  15.0 22.7 %while.168 = (s32[]{:T(128)}, f32[512]{0:T(512)S(1)}, f32[512]{0:T(512)S(1)}, f32[4,2048]{1,0:T(4,128)S(1)}, bf16[4,2048,128]{2,1,0:T(8,128)(2,1)S(1)}, /*index=5*/bf16[512,128]{1,0:T(8,128)(2,1)S(1)}, s32[]{:T(128)}, s32[]{:T(128)}) while((s32[]{:T(128)}, f32[512]{0:T(512)S(1)}, f32[512]{0:T(512)S(1)}, f32[4,2048]{1,0:T(4,128)S(1)}, ...), condition=%wide.region_5.6_spmd.clone, body=%wide.region_2.5_spmd.clone.sunk | while | flops 275778048 | bytes 9095272 | solution.py:90
  15.0 2.8 fusion.75
  17.8 2.8 exponential_reduce_fusion.12
  20.7 2.8 fusion.75
  23.5 2.8 exponential_reduce_fusion.12
  26.4 2.8 fusion.75
  29.2 2.8 exponential_reduce_fusion.12
  32.0 2.8 fusion.75
  34.8 2.8 exponential_reduce_fusion.12
  37.7 6.2 %all-gather.7 = f32[4,1,512]{2,1,0:T(1,128)S(1)} all-gather(f32[1,1,512]{2,1,0:T(1,128)S(1)} %bitcast.200), channel_id=2, replica_groups=mesh['wide'=8,'narrow'=4] {'narrow'}, dimensions={0}, use_global_device_ids=true | all-gather | bytes 10240 | tf_op jit(solution)/shard_map/all_gather | solution.py:17
  43.9 5.5 %all-gather.8 = f32[4,1,512]{2,1,0:T(1,128)S(1)} all-gather(f32[1,1,512]{2,1,0:T(1,128)S(1)} %bitcast.219), channel_id=3, replica_groups=mesh['wide'=8,'narrow'=4] {'narrow'}, dimensions={0}, use_global_device_ids=true | all-gather | bytes 10240 | tf_op jit(solution)/shard_map/all_gather | solution.py:17
  49.6 7.3 %while.162 = (s32[]{:T(128)}, f32[4,2048]{1,0:T(4,128)S(1)}, f32[4,2048]{1,0:T(4,128)S(1)}, f32[512]{0:T(512)S(1)}, bf16[4,2048,128]{2,1,0:T(8,128)(2,1)S(1)}, /...) while((s32[]{:T(128)}, f32[4,2048]{1,0:T(4,128)S(1)}, f32[4,2048]{1,0:T(4,128)S(1)}, ...), condition=%wide.region_11.12_spmd, body=%wide.region_8.11_spmd.sunk | while | flops 275771392 | bytes 9103457 | solution.py:104
  49.6 0.9 fusion.71
  51.4 0.9 fusion.71
  53.2 0.9 fusion.71
  55.0 0.9 fusion.71
  56.9 31.4 %all-gather.9 = f32[8,1,8192]{2,1,0:T(1,128)S(1)} all-gather(f32[1,1,8192]{2,1,0:T(1,128)S(1)} %reshape.75), channel_id=1, replica_groups=mesh['wide'=8,'narrow'=4] {'wide'}, dimensions={0}, use_global_device_ids=true | all-gather | bytes 294912 | tf_op jit(solution)/shard_map/all_gather | solution.py:17
  88.6 30.7 %all-gather.10 = f32[8,1,8192]{2,1,0:T(1,128)S(1)} all-gather(f32[1,1,8192]{2,1,0:T(1,128)S(1)} %reshape.77), channel_id=1, replica_groups=mesh['wide'=8,'narrow'=4] {'wide'}, dimensions={0}, use_global_device_ids=true | all-gather | bytes 294912 | tf_op jit(solution)/shard_map/all_gather | solution.py:17
  119.5 0.8 while.163
  120.4 22.7 %while.169 = (s32[]{:T(128)}, f32[512]{0:T(512)S(1)}, f32[512]{0:T(512)S(1)}, f32[4,2048]{1,0:T(4,128)S(1)}, bf16[4,2048,128]{2,1,0:T(8,128)(2,1)S(1)}, /*index=5*/bf16[512,128]{1,0:T(8,128)(2,1)S(1)}, s32[]{:T(128)}, s32[]{:T(128)}) while((s32[]{:T(128)}, f32[512]{0:T(512)S(1)}, f32[512]{0:T(512)S(1)}, ...), condition=%wide.region_17.18_spmd.clone, body=%wide.region_14.17_spmd.clone.sunk | while | flops 275778048 | bytes 9095272 | solution.py:90
  120.4 2.8 fusion.78
  123.2 2.8 exponential_reduce_fusion.13
  126.1 2.8 fusion.78
  128.9 2.8 exponential_reduce_fusion.13
  131.7 2.8 fusion.78
  134.5 2.8 exponential_reduce_fusion.13
  137.4 2.8 fusion.78
  140.2 2.8 exponential_reduce_fusion.13
  143.1 5.2 %all-gather.11 = f32[4,1,512]{2,1,0:T(1,128)S(1)} all-gather(f32[1,1,512]{2,1,0:T(1,128)S(1)} %bitcast.199), channel_id=4, replica_groups=mesh['wide'=8,'narrow'=4] {'narrow'}, dimensions={0}, use_global_device_ids=true | all-gather | bytes 10240 | tf_op jit(solution)/shard_map/all_gather | solution.py:17
  148.3 5.2 %all-gather.12 = f32[4,1,512]{2,1,0:T(1,128)S(1)} all-gather(f32[1,1,512]{2,1,0:T(1,128)S(1)} %bitcast.218), channel_id=5, replica_groups=mesh['wide'=8,'narrow'=4] {'narrow'}, dimensions={0}, use_global_device_ids=true | all-gather | bytes 10240 | tf_op jit(solution)/shard_map/all_gather | solution.py:17
  153.6 7.3 %while.165 = (s32[]{:T(128)}, f32[4,2048]{1,0:T(4,128)S(1)}, f32[4,2048]{1,0:T(4,128)S(1)}, f32[512]{0:T(512)S(1)}, bf16[4,2048,128]{2,1,0:T(8,128)(2,1)S(1)}, /...) while((s32[]{:T(128)}, f32[4,2048]{1,0:T(4,128)S(1)}, f32[4,2048]{1,0:T(4,128)S(1)}, ...), condition=%wide.region_23.24_spmd, body=%wide.region_20.23_spmd.sunk | while | flops 275771392 | bytes 9103457 | solution.py:104
  153.7 0.9 fusion.73
  155.5 0.9 fusion.73
  157.3 0.9 fusion.73
  159.1 0.9 fusion.73
  161.0 30.8 %all-gather.13 = f32[8,1,8192]{2,1,0:T(1,128)S(1)} all-gather(f32[1,1,8192]{2,1,0:T(1,128)S(1)} %reshape.83), channel_id=1, replica_groups=mesh['wide'=8,'narrow'=4] {'wide'}, dimensions={0}, use_global_device_ids=true | all-gather | bytes 294912 | tf_op jit(solution)/shard_map/all_gather | solution.py:17
  192.0 30.9 %all-gather.14 = f32[8,1,8192]{2,1,0:T(1,128)S(1)} all-gather(f32[1,1,8192]{2,1,0:T(1,128)S(1)} %reshape.85), channel_id=1, replica_groups=mesh['wide'=8,'narrow'=4] {'wide'}, dimensions={0}, use_global_device_ids=true | all-gather | bytes 294912 | tf_op jit(solution)/shard_map/all_gather | solution.py:17
  223.1 0.8 while.166
  224.6 33.0 %while.170 = (s32[]{:T(128)}, f32[512]{0:T(512)S(1)}, f32[512]{0:T(512)S(1)}, bf16[4,2048,128]{2,1,0:T(8,128)(2,1)}, f32[4,2048]{1,0:T(4,128)S(1)}, /*index=5*/b...) while((s32[]{:T(128)}, f32[512]{0:T(512)S(1)}, ...), condition=%wide.region_29.30_spmd.clone, body=%wide.region_26.29_spmd.clone.sunk | while | flops 554699264 | bytes 31281820 | solution.py:117
  224.6 2.7 fusion.82
  227.4 3.1 exponential_reduce_fusion.14
  230.8 2.0 fusion.84
  232.9 2.7 fusion.82
  235.6 3.1 exponential_reduce_fusion.14
  239.0 2.1 fusion.84
  241.1 2.7 fusion.82
  243.8 3.1 exponential_reduce_fusion.14
  247.3 2.1 fusion.84
  249.4 2.7 fusion.82
  252.1 3.1 exponential_reduce_fusion.14
  255.5 2.1 fusion.84
  257.6 5.2 %all-gather.15 = f32[4,1,512]{2,1,0:T(1,128)S(1)} all-gather(f32[1,1,512]{2,1,0:T(1,128)S(1)} %bitcast.198), channel_id=6, replica_groups=mesh['wide'=8,'narrow'=4] {'narrow'}, dimensions={0}, use_global_device_ids=true | all-gather | bytes 10240 | tf_op jit(solution)/shard_map/all_gather | solution.py:17
  262.8 5.2 %all-gather.16 = f32[4,1,512]{2,1,0:T(1,128)S(1)} all-gather(f32[1,1,512]{2,1,0:T(1,128)S(1)} %bitcast.217), channel_id=7, replica_groups=mesh['wide'=8,'narrow'=4] {'narrow'}, dimensions={0}, use_global_device_ids=true | all-gather | bytes 10240 | tf_op jit(solution)/shard_map/all_gather | solution.py:17
  268.7 7.0 %while.171 = (s32[]{:T(128)}, f32[512,128]{1,0:T(8,128)S(1)}, f32[4,2048]{1,0:T(4,128)S(1)}, bf16[4,2048,128]{2,1,0:T(8,128)(2,1)S(1)}, bf16[512,128]{1,0:T(8,12...) while((s32[]{:T(128)}, f32[512,128]{1,0:T(8,128)S(1)}, f32[4,2048]{1,0:T(4,128)S(1)}, ...), condition=%wide.region_33.34_spmd.clone, body=%wide.region_32.33_spmd.clone.sunk | while | flops 543293440 | bytes 1731683 | solution.py:139
  268.8 1.7 fusion.88
  270.5 1.7 fusion.88
  272.3 1.7 fusion.88
  274.0 1.7 fusion.88
  275.8 7.3 %all-gather.6 = bf16[2048,128]{1,0:T(8,128)(2,1)S(1)} all-gather(bf16[512,128]{1,0:T(8,128)(2,1)S(1)} %convert_element_type.45), channel_id=8, replica_groups=mesh['wide'=8,'narrow'=4] {'narrow'}, dimensions={0}, use_global_device_ids=true | all-gather | bytes 655360 | tf_op jit(solution)/shard_map/all_gather | solution.py:11
  283.2 0.8 convert_subtract_fusion.1
  284.0 43.2 %reduce-scatter.2.cloned.1.call-done = bf16[1024,128]{1,0:T(8,128)(2,1)} async-done(((bf16[8192,128]{1,0:T(8,128)(2,1)}), bf16[1024,128]{1,0:T(8,128)(2,1)}) %reduce-scatter.2.cloned.1.call-update) | async-done | bytes 262160 | tf_op jit(solution)/shard_map/reduce_scatter | solution.py:123
  327.3 1.8 convert_subtract_fusion
  (196 shorter events, 13.8 us)
Async XLA Ops:
  7.2 7.5 %copy-start.1 = (bf16[512,128]{1,0:T(8,128)(2,1)S(1)}, bf16[512,128]{1,0:T(8,128)(2,1)}, u32[]{:S(2)}) copy-start(bf16[512,128]{1,0:T(8,128)(2,1)} %param.27) | copy-start | bytes 393220
  7.2 7.8 %copy-start.4 = (f32[8192]{0:T(1024)S(1)}, f32[8192]{0:T(1024)}, u32[]{:S(2)}) copy-start(f32[8192]{0:T(1024)} %param.31) | copy-start | bytes 98308
  7.2 320.1 %reduce-scatter.2.cloned.1.call-start = ((), (), s32[]{:S(2)}) async-start(), calls=%async_computation.1 | async-start | bytes 2359296 | tf_op jit(solution)/shard_map/reduce_scatter | solution.py:123
  15.0 34.5 %copy-start.5 = (f32[512]{0:T(512)S(1)}, f32[512]{0:T(512)}, u32[]{:S(2)}) copy-start(f32[512]{0:T(512)} %param.29) | copy-start | bytes 6148
  49.6 70.8 %copy-start.3 = (f32[8192]{0:T(1024)S(1)}, f32[8192]{0:T(1024)}, u32[]{:S(2)}) copy-start(f32[8192]{0:T(1024)} %param.30) | copy-start | bytes 98308
  224.0 0.6 copy-start.2
  227.3 3.4 %copy-start = (f32[2048,512]{1,0:T(8,128)S(1)}, f32[2048,512]{1,0:T(8,128)}, u32[]{:S(2)}) copy-start(f32[2048,512]{1,0:T(8,128)} %get-tuple-element.1612) | copy-start | bytes 12582916 | tf_op jit(solution)/shard_map/while
  235.6 3.4 %copy-start = (f32[2048,512]{1,0:T(8,128)S(1)}, f32[2048,512]{1,0:T(8,128)}, u32[]{:S(2)}) copy-start(f32[2048,512]{1,0:T(8,128)} %get-tuple-element.1612) | copy-start | bytes 12582916 | tf_op jit(solution)/shard_map/while
  243.8 3.4 %copy-start = (f32[2048,512]{1,0:T(8,128)S(1)}, f32[2048,512]{1,0:T(8,128)}, u32[]{:S(2)}) copy-start(f32[2048,512]{1,0:T(8,128)} %get-tuple-element.1612) | copy-start | bytes 12582916 | tf_op jit(solution)/shard_map/while
  252.1 3.4 %copy-start = (f32[2048,512]{1,0:T(8,128)S(1)}, f32[2048,512]{1,0:T(8,128)}, u32[]{:S(2)}) copy-start(f32[2048,512]{1,0:T(8,128)} %get-tuple-element.1612) | copy-start | bytes 12582916 | tf_op jit(solution)/shard_map/while
Sparse Core Ops, SparseCore 0:
  257.7 69.4 reduce-scatter.1
